TPU v7x, 128 devices: a whole 4x4x4 slice. The times are simulated.
128 devices in a mesh: gx: 8 (over y, core), gy: 16 (over z, x).
Axes of the slice: x: 4, y: 4, z: 4, core: 2. Of those that a mesh axis runs over, the one named last changes fastest.
Arguments:
- trace_op: bfloat16 [8, 16, 2048, 2048], P('gx', 'gy'), may hold values from -0.125 to 0.125
- src_blocks: bfloat16 [16384, 2048], P(('gx', 'gy')), may hold values from -6 to 6
- src_dest: int32 [16384, 1], P(('gx', 'gy')), may hold values from 0 to 127; in each aligned block of 128 rows (0 to 127, 128 to 255, ...) at most 2 rows name the same one
- src_shot: int32 [16384], P(('gx', 'gy')), may hold values from 0 to 2047
- ret_shot: int32 [128, 128, 4], P(('gx', 'gy')), may hold values from 0 to 2047
- ret_count: int32 [128, 128], P(('gx', 'gy')), may hold values from 0 to 4
Outputs:
- returned: bfloat16 [128, 128, 4, 2048], P(('gx', 'gy'))
Inputs may be any that keep to these rules, and one draw needn't show every extreme that they name: `src_dest`: among the rows of one device, no subdomain is named by more than 2 blocks; some subdomain is named by exactly 2.
All inputs are finite; a program needn't handle non-finite values.
Results may differ from a plain program's by a relative error of at most 0.013.
Values may be sent and summed in bfloat16 or wider, within the bound.
A program may use at most 128 MiB of HBM per device.

v0:
```python
import jax
import jax.numpy as jnp
from jax import lax
from jax.sharding import PartitionSpec as P

S = 256
BATCHES = 8
RCAP = 4


def shifted(array, axis, by):
    devices = lax.axis_size(axis)
    pairs = [(i, i + by) for i in range(devices) if 0 <= i + by < devices]
    return lax.ppermute(array, axis, pairs)


def body(trace_op, src_blocks, src_dest, src_shot, ret_shot, ret_count):
    cols = lax.axis_size("gx")
    rows_axis = lax.axis_size("gy")
    ndev = cols * rows_axis
    blk = src_blocks.shape[0]
    width = src_blocks.shape[1]
    face = width // 2
    scap = max(2, 2 * blk // ndev)
    shots = S * BATCHES
    dest = src_dest[:, 0]
    hits = (dest[:, None] == jnp.arange(ndev, dtype=jnp.int32)[None, :]).astype(jnp.int32)
    ranks = jnp.sum((jnp.cumsum(hits, axis=0) - 1) * hits, axis=1)
    target = dest * scap + ranks
    place = jnp.arange(ndev * scap, dtype=jnp.int32)[:, None] == target[None, :]
    packed = jnp.dot(
        place.astype(jnp.bfloat16), src_blocks, preferred_element_type=jnp.float32
    ).astype(jnp.bfloat16)
    slot_shots = jnp.max(jnp.where(place, src_shot[None, :], -1), axis=1)
    recv_blocks, recv_shots = (
        lax.all_to_all(
            packed.reshape(ndev, scap, width), ("gx", "gy"), split_axis=0, concat_axis=0, tiled=True
        ),
        lax.all_to_all(
            slot_shots.reshape(ndev, scap), ("gx", "gy"), split_axis=0, concat_axis=0, tiled=True
        ),
    )
    recv_blocks = recv_blocks.reshape(ndev * scap, width)
    recv_shots = recv_shots.reshape(ndev * scap)
    selector = (jnp.arange(shots, dtype=jnp.int32)[:, None] == recv_shots[None, :]).astype(
        jnp.bfloat16
    )
    source = jnp.dot(selector, recv_blocks, preferred_element_type=jnp.float32)
    split = 1
    block = S // split
    count = BATCHES * split
    operator = trace_op.reshape(width, width)
    upper_rows = operator[:face]
    lower_rows = operator[face:]
    column_index = lax.axis_index("gx")
    row_index = lax.axis_index("gy")
    ticks = cols + rows_axis - 2 + count

    def tick(step, carry):
        left, lower, traces = carry
        offset = step - (column_index + row_index)
        active = (offset >= 0) & (offset < count)
        where = jnp.clip(offset, 0, count - 1) * block

        def compute(unused):
            term = lax.dynamic_slice_in_dim(source, where, block, 0)
            total = jnp.dot(left, upper_rows, preferred_element_type=jnp.float32)
            total = total + jnp.dot(lower, lower_rows, preferred_element_type=jnp.float32)
            result = (total + term).astype(jnp.bfloat16)
            return (result, lax.dynamic_update_slice_in_dim(traces, result, where, 0))

        def skip(unused):
            return (jnp.zeros((block, width), jnp.bfloat16), traces)

        result, traces = lax.cond(active, compute, skip, None)
        left = shifted(result[:, :face], "gx", 1)
        lower = shifted(result[:, face:], "gy", 1)
        return (left, lower, traces)

    start = (
        jnp.zeros((block, face), jnp.bfloat16),
        jnp.zeros((block, face), jnp.bfloat16),
        jnp.zeros((shots, width), jnp.bfloat16),
    )
    _, _, traces = lax.fori_loop(0, ticks, tick, start)
    wanted = ret_shot.reshape(ndev * RCAP)
    chosen = jnp.take(traces, wanted, axis=0)
    live = (jnp.arange(RCAP, dtype=jnp.int32)[None, :] < ret_count.reshape(ndev, 1)).reshape(
        ndev * RCAP
    )
    chosen = jnp.where(live[:, None], chosen, jnp.zeros_like(chosen))
    arrived = lax.all_to_all(
        chosen.reshape(ndev, RCAP, width), ("gx", "gy"), split_axis=0, concat_axis=0, tiled=True
    )
    return arrived.reshape(1, ndev, RCAP, width)


def solution(mesh):
    in_specs = (
        P("gx", "gy", None, None),
        P(("gx", "gy"), None),
        P(("gx", "gy"), None),
        P(("gx", "gy")),
        P(("gx", "gy"), None, None),
        P(("gx", "gy"), None),
    )
    out_specs = P(("gx", "gy"), None, None, None)
    return jax.shard_map(body, mesh=mesh, in_specs=in_specs, out_specs=out_specs, check_vma=False)
```

profile of v0, /device:TPU:97, one launch (start us, length us, event | category | flops | bytes accessed | tf_op | source)
XLA Modules:
  0.0 716.7 jit_solution(12706773894705315802)
XLA Ops:
  4.0 10.1 %all-to-all-start = ((s32[128,1,2]{2,1,0:T(1,128)}), s32[128,1,2]{2,1,0:T(1,128)S(1)}, u32[]{:S(2)}, u32[]{:S(2)}) async-start(s32[128,1,2]{2,1,0:T(1,128)} %bitcast.5), calls=%async_computation | async-start | bytes 131072 | tf_op jit(solution)/shard_map/all_to_all | solution.py:39
  58.6 606.7 %while.22 = (s32[]{:T(128)}, bf16[256,1024]{1,0:T(8,128)(2,1)}, bf16[256,1024]{1,0:T(8,128)(2,1)S(1)}, bf16[2048,2048]{1,0:T(8,128)(2,1)}, s32[]{:T(128)}, /*ind...) while((s32[]{:T(128)}, bf16[256,1024]{1,0:T(8,128)(2,1)}, ...), condition=%wide.region_6.7_spmd, body=%wide.region_3.6_spmd.sunk | while | flops 2149056512 | bytes 40894864 | solution.py:85
  67.3 10.5 %collective-permute-done.1 = bf16[256,1024]{1,0:T(8,128)(2,1)S(1)} collective-permute-done((bf16[256,1024]{1,0:T(8,128)(2,1)S(1)}, bf16[256,1024]{1,0:T(8,128)(2,1)S(1)}, u32[]{:S(2)}, u32[]{:S(2)}) %collective-permute-start.1) | collective-permute-done | bytes 524320 | tf_op jit(solution)/shard_map/while/body/eval_jaxpr/ppermute | solution.py:14
  87.5 11.0 %collective-permute-done.1 = bf16[256,1024]{1,0:T(8,128)(2,1)S(1)} collective-permute-done((bf16[256,1024]{1,0:T(8,128)(2,1)S(1)}, bf16[256,1024]{1,0:T(8,128)(2,1)S(1)}, u32[]{:S(2)}, u32[]{:S(2)}) %collective-permute-start.1) | collective-permute-done | bytes 524320 | tf_op jit(solution)/shard_map/while/body/eval_jaxpr/ppermute | solution.py:14
  107.6 10.8 %collective-permute-done.1 = bf16[256,1024]{1,0:T(8,128)(2,1)S(1)} collective-permute-done((bf16[256,1024]{1,0:T(8,128)(2,1)S(1)}, bf16[256,1024]{1,0:T(8,128)(2,1)S(1)}, u32[]{:S(2)}, u32[]{:S(2)}) %collective-permute-start.1) | collective-permute-done | bytes 524320 | tf_op jit(solution)/shard_map/while/body/eval_jaxpr/ppermute | solution.py:14
  129.2 11.1 %collective-permute-done.1 = bf16[256,1024]{1,0:T(8,128)(2,1)S(1)} collective-permute-done((bf16[256,1024]{1,0:T(8,128)(2,1)S(1)}, bf16[256,1024]{1,0:T(8,128)(2,1)S(1)}, u32[]{:S(2)}, u32[]{:S(2)}) %collective-permute-start.1) | collective-permute-done | bytes 524320 | tf_op jit(solution)/shard_map/while/body/eval_jaxpr/ppermute | solution.py:14
  149.3 10.8 %collective-permute-done.1 = bf16[256,1024]{1,0:T(8,128)(2,1)S(1)} collective-permute-done((bf16[256,1024]{1,0:T(8,128)(2,1)S(1)}, bf16[256,1024]{1,0:T(8,128)(2,1)S(1)}, u32[]{:S(2)}, u32[]{:S(2)}) %collective-permute-start.1) | collective-permute-done | bytes 524320 | tf_op jit(solution)/shard_map/while/body/eval_jaxpr/ppermute | solution.py:14
  168.4 9.9 %collective-permute-done.1 = bf16[256,1024]{1,0:T(8,128)(2,1)S(1)} collective-permute-done((bf16[256,1024]{1,0:T(8,128)(2,1)S(1)}, bf16[256,1024]{1,0:T(8,128)(2,1)S(1)}, u32[]{:S(2)}, u32[]{:S(2)}) %collective-permute-start.1) | collective-permute-done | bytes 524320 | tf_op jit(solution)/shard_map/while/body/eval_jaxpr/ppermute | solution.py:14
  186.7 9.0 %collective-permute-done.1 = bf16[256,1024]{1,0:T(8,128)(2,1)S(1)} collective-permute-done((bf16[256,1024]{1,0:T(8,128)(2,1)S(1)}, bf16[256,1024]{1,0:T(8,128)(2,1)S(1)}, u32[]{:S(2)}, u32[]{:S(2)}) %collective-permute-start.1) | collective-permute-done | bytes 524320 | tf_op jit(solution)/shard_map/while/body/eval_jaxpr/ppermute | solution.py:14
  281.4 33.2 %collective-permute-done = bf16[256,1024]{1,0:T(8,128)(2,1)} collective-permute-done((bf16[256,1024]{1,0:T(8,128)(2,1)S(1)}, bf16[256,1024]{1,0:T(8,128)(2,1)}, u32[]{:S(2)}, u32[]{:S(2)}) %collective-permute-start) | collective-permute-done | bytes 524320 | tf_op jit(solution)/shard_map/while/body/eval_jaxpr/ppermute | solution.py:14
  326.2 11.8 %collective-permute-done = bf16[256,1024]{1,0:T(8,128)(2,1)} collective-permute-done((bf16[256,1024]{1,0:T(8,128)(2,1)S(1)}, bf16[256,1024]{1,0:T(8,128)(2,1)}, u32[]{:S(2)}, u32[]{:S(2)}) %collective-permute-start) | collective-permute-done | bytes 524320 | tf_op jit(solution)/shard_map/while/body/eval_jaxpr/ppermute | solution.py:14
  350.8 10.3 %collective-permute-done = bf16[256,1024]{1,0:T(8,128)(2,1)} collective-permute-done((bf16[256,1024]{1,0:T(8,128)(2,1)S(1)}, bf16[256,1024]{1,0:T(8,128)(2,1)}, u32[]{:S(2)}, u32[]{:S(2)}) %collective-permute-start) | collective-permute-done | bytes 524320 | tf_op jit(solution)/shard_map/while/body/eval_jaxpr/ppermute | solution.py:14
  374.2 10.1 %collective-permute-done = bf16[256,1024]{1,0:T(8,128)(2,1)} collective-permute-done((bf16[256,1024]{1,0:T(8,128)(2,1)S(1)}, bf16[256,1024]{1,0:T(8,128)(2,1)}, u32[]{:S(2)}, u32[]{:S(2)}) %collective-permute-start) | collective-permute-done | bytes 524320 | tf_op jit(solution)/shard_map/while/body/eval_jaxpr/ppermute | solution.py:14
  397.1 10.3 %collective-permute-done = bf16[256,1024]{1,0:T(8,128)(2,1)} collective-permute-done((bf16[256,1024]{1,0:T(8,128)(2,1)S(1)}, bf16[256,1024]{1,0:T(8,128)(2,1)}, u32[]{:S(2)}, u32[]{:S(2)}) %collective-permute-start) | collective-permute-done | bytes 524320 | tf_op jit(solution)/shard_map/while/body/eval_jaxpr/ppermute | solution.py:14
  420.1 10.4 %collective-permute-done = bf16[256,1024]{1,0:T(8,128)(2,1)} collective-permute-done((bf16[256,1024]{1,0:T(8,128)(2,1)S(1)}, bf16[256,1024]{1,0:T(8,128)(2,1)}, u32[]{:S(2)}, u32[]{:S(2)}) %collective-permute-start) | collective-permute-done | bytes 524320 | tf_op jit(solution)/shard_map/while/body/eval_jaxpr/ppermute | solution.py:14
  443.1 10.6 %collective-permute-done = bf16[256,1024]{1,0:T(8,128)(2,1)} collective-permute-done((bf16[256,1024]{1,0:T(8,128)(2,1)S(1)}, bf16[256,1024]{1,0:T(8,128)(2,1)}, u32[]{:S(2)}, u32[]{:S(2)}) %collective-permute-start) | collective-permute-done | bytes 524320 | tf_op jit(solution)/shard_map/while/body/eval_jaxpr/ppermute | solution.py:14
  466.0 10.8 %collective-permute-done = bf16[256,1024]{1,0:T(8,128)(2,1)} collective-permute-done((bf16[256,1024]{1,0:T(8,128)(2,1)S(1)}, bf16[256,1024]{1,0:T(8,128)(2,1)}, u32[]{:S(2)}, u32[]{:S(2)}) %collective-permute-start) | collective-permute-done | bytes 524320 | tf_op jit(solution)/shard_map/while/body/eval_jaxpr/ppermute | solution.py:14
  500.7 9.3 %collective-permute-start = (bf16[256,1024]{1,0:T(8,128)(2,1)S(1)}, bf16[256,1024]{1,0:T(8,128)(2,1)}, u32[]{:S(2)}, u32[]{:S(2)}) collective-permute-start(bf16[256,1024]{1,0:T(8,128)(2,1)S(1)} %get-tuple-element.341), channel_id=1, source_target_pairs={{0,16},{16,32},{32,48},{48,64},{64,80},{80,96},{96,112},{1,17},{17... | collective-permute-start | bytes 1572872 | tf_op jit(solution)/shard_map/while/body/eval_jaxpr/ppermute | solution.py:14
  516.1 10.0 %collective-permute-done.1 = bf16[256,1024]{1,0:T(8,128)(2,1)S(1)} collective-permute-done((bf16[256,1024]{1,0:T(8,128)(2,1)S(1)}, bf16[256,1024]{1,0:T(8,128)(2,1)S(1)}, u32[]{:S(2)}, u32[]{:S(2)}) %collective-permute-start.1) | collective-permute-done | bytes 524320 | tf_op jit(solution)/shard_map/while/body/eval_jaxpr/ppermute | solution.py:14
  534.4 10.1 %collective-permute-done.1 = bf16[256,1024]{1,0:T(8,128)(2,1)S(1)} collective-permute-done((bf16[256,1024]{1,0:T(8,128)(2,1)S(1)}, bf16[256,1024]{1,0:T(8,128)(2,1)S(1)}, u32[]{:S(2)}, u32[]{:S(2)}) %collective-permute-start.1) | collective-permute-done | bytes 524320 | tf_op jit(solution)/shard_map/while/body/eval_jaxpr/ppermute | solution.py:14
  552.7 9.1 %collective-permute-done.1 = bf16[256,1024]{1,0:T(8,128)(2,1)S(1)} collective-permute-done((bf16[256,1024]{1,0:T(8,128)(2,1)S(1)}, bf16[256,1024]{1,0:T(8,128)(2,1)S(1)}, u32[]{:S(2)}, u32[]{:S(2)}) %collective-permute-start.1) | collective-permute-done | bytes 524320 | tf_op jit(solution)/shard_map/while/body/eval_jaxpr/ppermute | solution.py:14
  635.9 11.0 %collective-permute-done.1 = bf16[256,1024]{1,0:T(8,128)(2,1)S(1)} collective-permute-done((bf16[256,1024]{1,0:T(8,128)(2,1)S(1)}, bf16[256,1024]{1,0:T(8,128)(2,1)S(1)}, u32[]{:S(2)}, u32[]{:S(2)}) %collective-permute-start.1) | collective-permute-done | bytes 524320 | tf_op jit(solution)/shard_map/while/body/eval_jaxpr/ppermute | solution.py:14
  655.2 10.1 %collective-permute-done.1 = bf16[256,1024]{1,0:T(8,128)(2,1)S(1)} collective-permute-done((bf16[256,1024]{1,0:T(8,128)(2,1)S(1)}, bf16[256,1024]{1,0:T(8,128)(2,1)S(1)}, u32[]{:S(2)}, u32[]{:S(2)}) %collective-permute-start.1) | collective-permute-done | bytes 524320 | tf_op jit(solution)/shard_map/while/body/eval_jaxpr/ppermute | solution.py:14
  678.9 36.4 %all_to_all.19 = bf16[128,4,2048]{2,1,0:T(4,128)(2,1)S(1)} all-to-all(bf16[128,4,2048]{2,1,0:T(4,128)(2,1)S(1)} %select_select_fusion), channel_id=1, replica_groups=mesh['gx'=8,'gy'=16] {'gx','gy'}, dimensions={0} | all-to-all | bytes 4194304 | tf_op jit(solution)/shard_map/all_to_all | solution.py:92
  (248 shorter events, 493.2 us)
Async XLA Ops:
  4.0 17.2 %all-to-all-start = ((s32[128,1,2]{2,1,0:T(1,128)}), s32[128,1,2]{2,1,0:T(1,128)S(1)}, u32[]{:S(2)}, u32[]{:S(2)}) async-start(s32[128,1,2]{2,1,0:T(1,128)} %bitcast.5), calls=%async_computation | async-start | bytes 131072 | tf_op jit(solution)/shard_map/all_to_all | solution.py:39
  21.2 23.7 %all-to-all-start.1 = ((bf16[128,2,2048]{2,1,0:T(2,128)(2,1)}), bf16[128,2,2048]{2,1,0:T(2,128)(2,1)S(1)}, u32[]{:S(2)}, u32[]{:S(2)}) async-start(bf16[128,2,2048]{2,1,0:T(2,128)(2,1)} %reshape.92), calls=%async_computation.1 | async-start | bytes 2097152 | tf_op jit(solution)/shard_map/all_to_all | solution.py:36
  61.2 16.6 %collective-permute-start.1 = (bf16[256,1024]{1,0:T(8,128)(2,1)S(1)}, bf16[256,1024]{1,0:T(8,128)(2,1)S(1)}, u32[]{:S(2)}, u32[]{:S(2)}) collective-permute-start(bf16[256,1024]{1,0:T(8,128)(2,1)S(1)} %get-tuple-element.342), channel_id=1, source_target_pairs={{0,1},{1,2},{2,3},{3,4},{4,5},{5,6},{6,7},{7,8},{8,9},{9,10},{10,1... | collective-permute-start | bytes 1572872 | tf_op jit(solution)/shard_map/while/body/eval_jaxpr/ppermute | solution.py:14
  81.4 17.1 %collective-permute-start.1 = (bf16[256,1024]{1,0:T(8,128)(2,1)S(1)}, bf16[256,1024]{1,0:T(8,128)(2,1)S(1)}, u32[]{:S(2)}, u32[]{:S(2)}) collective-permute-start(bf16[256,1024]{1,0:T(8,128)(2,1)S(1)} %get-tuple-element.342), channel_id=1, source_target_pairs={{0,1},{1,2},{2,3},{3,4},{4,5},{5,6},{6,7},{7,8},{8,9},{9,10},{10,1... | collective-permute-start | bytes 1572872 | tf_op jit(solution)/shard_map/while/body/eval_jaxpr/ppermute | solution.py:14
  101.5 16.9 %collective-permute-start.1 = (bf16[256,1024]{1,0:T(8,128)(2,1)S(1)}, bf16[256,1024]{1,0:T(8,128)(2,1)S(1)}, u32[]{:S(2)}, u32[]{:S(2)}) collective-permute-start(bf16[256,1024]{1,0:T(8,128)(2,1)S(1)} %get-tuple-element.342), channel_id=1, source_target_pairs={{0,1},{1,2},{2,3},{3,4},{4,5},{5,6},{6,7},{7,8},{8,9},{9,10},{10,1... | collective-permute-start | bytes 1572872 | tf_op jit(solution)/shard_map/while/body/eval_jaxpr/ppermute | solution.py:14
  123.1 17.2 %collective-permute-start.1 = (bf16[256,1024]{1,0:T(8,128)(2,1)S(1)}, bf16[256,1024]{1,0:T(8,128)(2,1)S(1)}, u32[]{:S(2)}, u32[]{:S(2)}) collective-permute-start(bf16[256,1024]{1,0:T(8,128)(2,1)S(1)} %get-tuple-element.342), channel_id=1, source_target_pairs={{0,1},{1,2},{2,3},{3,4},{4,5},{5,6},{6,7},{7,8},{8,9},{9,10},{10,1... | collective-permute-start | bytes 1572872 | tf_op jit(solution)/shard_map/while/body/eval_jaxpr/ppermute | solution.py:14
  143.1 16.9 %collective-permute-start.1 = (bf16[256,1024]{1,0:T(8,128)(2,1)S(1)}, bf16[256,1024]{1,0:T(8,128)(2,1)S(1)}, u32[]{:S(2)}, u32[]{:S(2)}) collective-permute-start(bf16[256,1024]{1,0:T(8,128)(2,1)S(1)} %get-tuple-element.342), channel_id=1, source_target_pairs={{0,1},{1,2},{2,3},{3,4},{4,5},{5,6},{6,7},{7,8},{8,9},{9,10},{10,1... | collective-permute-start | bytes 1572872 | tf_op jit(solution)/shard_map/while/body/eval_jaxpr/ppermute | solution.py:14
  162.3 16.0 %collective-permute-start.1 = (bf16[256,1024]{1,0:T(8,128)(2,1)S(1)}, bf16[256,1024]{1,0:T(8,128)(2,1)S(1)}, u32[]{:S(2)}, u32[]{:S(2)}) collective-permute-start(bf16[256,1024]{1,0:T(8,128)(2,1)S(1)} %get-tuple-element.342), channel_id=1, source_target_pairs={{0,1},{1,2},{2,3},{3,4},{4,5},{5,6},{6,7},{7,8},{8,9},{9,10},{10,1... | collective-permute-start | bytes 1572872 | tf_op jit(solution)/shard_map/while/body/eval_jaxpr/ppermute | solution.py:14
  180.6 15.1 %collective-permute-start.1 = (bf16[256,1024]{1,0:T(8,128)(2,1)S(1)}, bf16[256,1024]{1,0:T(8,128)(2,1)S(1)}, u32[]{:S(2)}, u32[]{:S(2)}) collective-permute-start(bf16[256,1024]{1,0:T(8,128)(2,1)S(1)} %get-tuple-element.342), channel_id=1, source_target_pairs={{0,1},{1,2},{2,3},{3,4},{4,5},{5,6},{6,7},{7,8},{8,9},{9,10},{10,1... | collective-permute-start | bytes 1572872 | tf_op jit(solution)/shard_map/while/body/eval_jaxpr/ppermute | solution.py:14
  273.3 41.2 %collective-permute-start = (bf16[256,1024]{1,0:T(8,128)(2,1)S(1)}, bf16[256,1024]{1,0:T(8,128)(2,1)}, u32[]{:S(2)}, u32[]{:S(2)}) collective-permute-start(bf16[256,1024]{1,0:T(8,128)(2,1)S(1)} %get-tuple-element.341), channel_id=1, source_target_pairs={{0,16},{16,32},{32,48},{48,64},{64,80},{80,96},{96,112},{1,17},{17... | collective-permute-start | bytes 1572872 | tf_op jit(solution)/shard_map/while/body/eval_jaxpr/ppermute | solution.py:14
  279.5 35.1 %collective-permute-start.1 = (bf16[256,1024]{1,0:T(8,128)(2,1)S(1)}, bf16[256,1024]{1,0:T(8,128)(2,1)S(1)}, u32[]{:S(2)}, u32[]{:S(2)}) collective-permute-start(bf16[256,1024]{1,0:T(8,128)(2,1)S(1)} %get-tuple-element.342), channel_id=1, source_target_pairs={{0,1},{1,2},{2,3},{3,4},{4,5},{5,6},{6,7},{7,8},{8,9},{9,10},{10,1... | collective-permute-start | bytes 1572872 | tf_op jit(solution)/shard_map/while/body/eval_jaxpr/ppermute | solution.py:14
  322.4 15.6 %collective-permute-start = (bf16[256,1024]{1,0:T(8,128)(2,1)S(1)}, bf16[256,1024]{1,0:T(8,128)(2,1)}, u32[]{:S(2)}, u32[]{:S(2)}) collective-permute-start(bf16[256,1024]{1,0:T(8,128)(2,1)S(1)} %get-tuple-element.341), channel_id=1, source_target_pairs={{0,16},{16,32},{32,48},{48,64},{64,80},{80,96},{96,112},{1,17},{17... | collective-permute-start | bytes 1572872 | tf_op jit(solution)/shard_map/while/body/eval_jaxpr/ppermute | solution.py:14
  346.1 15.0 %collective-permute-start = (bf16[256,1024]{1,0:T(8,128)(2,1)S(1)}, bf16[256,1024]{1,0:T(8,128)(2,1)}, u32[]{:S(2)}, u32[]{:S(2)}) collective-permute-start(bf16[256,1024]{1,0:T(8,128)(2,1)S(1)} %get-tuple-element.341), channel_id=1, source_target_pairs={{0,16},{16,32},{32,48},{48,64},{64,80},{80,96},{96,112},{1,17},{17... | collective-permute-start | bytes 1572872 | tf_op jit(solution)/shard_map/while/body/eval_jaxpr/ppermute | solution.py:14
  369.4 14.9 %collective-permute-start = (bf16[256,1024]{1,0:T(8,128)(2,1)S(1)}, bf16[256,1024]{1,0:T(8,128)(2,1)}, u32[]{:S(2)}, u32[]{:S(2)}) collective-permute-start(bf16[256,1024]{1,0:T(8,128)(2,1)S(1)} %get-tuple-element.341), channel_id=1, source_target_pairs={{0,16},{16,32},{32,48},{48,64},{64,80},{80,96},{96,112},{1,17},{17... | collective-permute-start | bytes 1572872 | tf_op jit(solution)/shard_map/while/body/eval_jaxpr/ppermute | solution.py:14
  392.3 15.1 %collective-permute-start = (bf16[256,1024]{1,0:T(8,128)(2,1)S(1)}, bf16[256,1024]{1,0:T(8,128)(2,1)}, u32[]{:S(2)}, u32[]{:S(2)}) collective-permute-start(bf16[256,1024]{1,0:T(8,128)(2,1)S(1)} %get-tuple-element.341), channel_id=1, source_target_pairs={{0,16},{16,32},{32,48},{48,64},{64,80},{80,96},{96,112},{1,17},{17... | collective-permute-start | bytes 1572872 | tf_op jit(solution)/shard_map/while/body/eval_jaxpr/ppermute | solution.py:14
  415.2 15.3 %collective-permute-start = (bf16[256,1024]{1,0:T(8,128)(2,1)S(1)}, bf16[256,1024]{1,0:T(8,128)(2,1)}, u32[]{:S(2)}, u32[]{:S(2)}) collective-permute-start(bf16[256,1024]{1,0:T(8,128)(2,1)S(1)} %get-tuple-element.341), channel_id=1, source_target_pairs={{0,16},{16,32},{32,48},{48,64},{64,80},{80,96},{96,112},{1,17},{17... | collective-permute-start | bytes 1572872 | tf_op jit(solution)/shard_map/while/body/eval_jaxpr/ppermute | solution.py:14
  438.4 15.3 %collective-permute-start = (bf16[256,1024]{1,0:T(8,128)(2,1)S(1)}, bf16[256,1024]{1,0:T(8,128)(2,1)}, u32[]{:S(2)}, u32[]{:S(2)}) collective-permute-start(bf16[256,1024]{1,0:T(8,128)(2,1)S(1)} %get-tuple-element.341), channel_id=1, source_target_pairs={{0,16},{16,32},{32,48},{48,64},{64,80},{80,96},{96,112},{1,17},{17... | collective-permute-start | bytes 1572872 | tf_op jit(solution)/shard_map/while/body/eval_jaxpr/ppermute | solution.py:14
  461.5 15.3 %collective-permute-start = (bf16[256,1024]{1,0:T(8,128)(2,1)S(1)}, bf16[256,1024]{1,0:T(8,128)(2,1)}, u32[]{:S(2)}, u32[]{:S(2)}) collective-permute-start(bf16[256,1024]{1,0:T(8,128)(2,1)S(1)} %get-tuple-element.341), channel_id=1, source_target_pairs={{0,16},{16,32},{32,48},{48,64},{64,80},{80,96},{96,112},{1,17},{17... | collective-permute-start | bytes 1572872 | tf_op jit(solution)/shard_map/while/body/eval_jaxpr/ppermute | solution.py:14
  500.7 15.5 %collective-permute-start = (bf16[256,1024]{1,0:T(8,128)(2,1)S(1)}, bf16[256,1024]{1,0:T(8,128)(2,1)}, u32[]{:S(2)}, u32[]{:S(2)}) collective-permute-start(bf16[256,1024]{1,0:T(8,128)(2,1)S(1)} %get-tuple-element.341), channel_id=1, source_target_pairs={{0,16},{16,32},{32,48},{48,64},{64,80},{80,96},{96,112},{1,17},{17... | collective-permute-start | bytes 1572872 | tf_op jit(solution)/shard_map/while/body/eval_jaxpr/ppermute | solution.py:14
  510.0 16.1 %collective-permute-start.1 = (bf16[256,1024]{1,0:T(8,128)(2,1)S(1)}, bf16[256,1024]{1,0:T(8,128)(2,1)S(1)}, u32[]{:S(2)}, u32[]{:S(2)}) collective-permute-start(bf16[256,1024]{1,0:T(8,128)(2,1)S(1)} %get-tuple-element.342), channel_id=1, source_target_pairs={{0,1},{1,2},{2,3},{3,4},{4,5},{5,6},{6,7},{7,8},{8,9},{9,10},{10,1... | collective-permute-start | bytes 1572872 | tf_op jit(solution)/shard_map/while/body/eval_jaxpr/ppermute | solution.py:14
  528.3 16.2 %collective-permute-start.1 = (bf16[256,1024]{1,0:T(8,128)(2,1)S(1)}, bf16[256,1024]{1,0:T(8,128)(2,1)S(1)}, u32[]{:S(2)}, u32[]{:S(2)}) collective-permute-start(bf16[256,1024]{1,0:T(8,128)(2,1)S(1)} %get-tuple-element.342), channel_id=1, source_target_pairs={{0,1},{1,2},{2,3},{3,4},{4,5},{5,6},{6,7},{7,8},{8,9},{9,10},{10,1... | collective-permute-start | bytes 1572872 | tf_op jit(solution)/shard_map/while/body/eval_jaxpr/ppermute | solution.py:14
  546.6 15.2 %collective-permute-start.1 = (bf16[256,1024]{1,0:T(8,128)(2,1)S(1)}, bf16[256,1024]{1,0:T(8,128)(2,1)S(1)}, u32[]{:S(2)}, u32[]{:S(2)}) collective-permute-start(bf16[256,1024]{1,0:T(8,128)(2,1)S(1)} %get-tuple-element.342), channel_id=1, source_target_pairs={{0,1},{1,2},{2,3},{3,4},{4,5},{5,6},{6,7},{7,8},{8,9},{9,10},{10,1... | collective-permute-start | bytes 1572872 | tf_op jit(solution)/shard_map/while/body/eval_jaxpr/ppermute | solution.py:14
  629.7 17.2 %collective-permute-start.1 = (bf16[256,1024]{1,0:T(8,128)(2,1)S(1)}, bf16[256,1024]{1,0:T(8,128)(2,1)S(1)}, u32[]{:S(2)}, u32[]{:S(2)}) collective-permute-start(bf16[256,1024]{1,0:T(8,128)(2,1)S(1)} %get-tuple-element.342), channel_id=1, source_target_pairs={{0,1},{1,2},{2,3},{3,4},{4,5},{5,6},{6,7},{7,8},{8,9},{9,10},{10,1... | collective-permute-start | bytes 1572872 | tf_op jit(solution)/shard_map/while/body/eval_jaxpr/ppermute | solution.py:14
  649.1 16.2 %collective-permute-start.1 = (bf16[256,1024]{1,0:T(8,128)(2,1)S(1)}, bf16[256,1024]{1,0:T(8,128)(2,1)S(1)}, u32[]{:S(2)}, u32[]{:S(2)}) collective-permute-start(bf16[256,1024]{1,0:T(8,128)(2,1)S(1)} %get-tuple-element.342), channel_id=1, source_target_pairs={{0,1},{1,2},{2,3},{3,4},{4,5},{5,6},{6,7},{7,8},{8,9},{9,10},{10,1... | collective-permute-start | bytes 1572872 | tf_op jit(solution)/shard_map/while/body/eval_jaxpr/ppermute | solution.py:14
  (48 other events, 474.0 us)
where the time goes:
time: 722 us; the launch traced here: 717 us
  waiting for transfers between devices  389 us (54%)
  starting transfers between devices  179 us (25%)
  matrix products  70.5 us (10%)
  blocking collectives  36.4 us (5%)
  local copies, waits for them, and re-layouts  32.7 us (5%)
  other arithmetic  7.36 us (1%)
    ppermute x60, waiting for transfers between devices, shifted(): return lax.ppermute(array, axis, pairs)  376 us
    ppermute x60, starting transfers between devices, shifted(): return lax.ppermute(array, axis, pairs)  162 us
    all_to_all x1, blocking collectives, body(): lax.all_to_all(chosen.reshape(ndev, RCAP, width), ('gx', 'gy'), split_axi...  36.4 us
    dot_general x8, matrix products, compute(): jnp.dot(lower, lower_rows, preferred_element_type=jnp.float32)  32.1 us
    dot_general x8, matrix products, compute(): total = jnp.dot(left, upper_rows, preferred_element_type=jnp.float32)  29.9 us
  transfers between devices with their start and end apart: 62, of which 56 were waited for; matrix products, arithmetic and copies ran while one was open for 2% of the time, Pallas kernels for 0%

commit v1 on v0

v1 whole, which is shorter than its diff:
```python
import functools

import jax
import jax.numpy as jnp
from jax import lax
from jax.experimental import pallas as pl
from jax.experimental.pallas import tpu as pltpu
from jax.sharding import PartitionSpec as P

MESH = pl.DeviceIdType.MESH
CHUNK = 32
RCAP = 4


def sweep(cols, rows, w_hbm, blocks, shots, want, out, w, xbuf, traces, wsem, send_r, recv_r, send_u, recv_u):
    i = lax.axis_index("gx")
    j = lax.axis_index("gy")
    total, width = traces.shape
    face = width // 2
    slots = blocks.shape[0]
    chunks = total // CHUNK
    load = pltpu.make_async_copy(w_hbm, w.at[pl.ds(0, width)], wsem)
    load.start()
    w[pl.ds(width, slots)] = blocks[...]

    @pl.when(i == 0)
    def _():
        xbuf[:, :face] = jnp.zeros((total, face), jnp.bfloat16)

    @pl.when(j == 0)
    def _():
        xbuf[:, face:] = jnp.zeros((total, face), jnp.bfloat16)

    load.wait()

    def right(k):
        at = pl.ds(pl.multiple_of(k * CHUNK, CHUNK), CHUNK)
        return pltpu.make_async_remote_copy(
            src_ref=traces.at[at, pl.ds(0, face)],
            dst_ref=xbuf.at[at, pl.ds(0, face)],
            send_sem=send_r.at[k],
            recv_sem=recv_r.at[k],
            device_id={"gx": lax.rem(i + 1, cols)},
            device_id_type=MESH,
        )

    def upper(k):
        at = pl.ds(pl.multiple_of(k * CHUNK, CHUNK), CHUNK)
        return pltpu.make_async_remote_copy(
            src_ref=traces.at[at, pl.ds(face, face)],
            dst_ref=xbuf.at[at, pl.ds(face, face)],
            send_sem=send_u.at[k],
            recv_sem=recv_u.at[k],
            device_id={"gy": lax.rem(j + 1, rows)},
            device_id_type=MESH,
        )

    def step(k, _):
        at = pl.ds(pl.multiple_of(k * CHUNK, CHUNK), CHUNK)
        number = lax.broadcasted_iota(jnp.int32, (CHUNK, slots), 0) + k * CHUNK
        pick = jnp.where(number == shots[...], 1.0, 0.0).astype(jnp.bfloat16)

        @pl.when(i > 0)
        def _():
            right(k).wait_recv()

        @pl.when(j > 0)
        def _():
            upper(k).wait_recv()

        x = jnp.concatenate([xbuf[at, :], pick], axis=1)
        traces[at, face:] = jnp.dot(x, w[:, face:], preferred_element_type=jnp.float32).astype(jnp.bfloat16)

        @pl.when(j < rows - 1)
        def _():
            upper(k).start()

        traces[at, :face] = jnp.dot(x, w[:, :face], preferred_element_type=jnp.float32).astype(jnp.bfloat16)

        @pl.when(i < cols - 1)
        def _():
            right(k).start()

        return 0

    lax.fori_loop(0, chunks, step, 0)
    number = lax.broadcasted_iota(jnp.int32, (128, total), 1)
    for part in range(want.shape[0] // 128):
        rows_at = pl.ds(part * 128, 128)
        pick = jnp.where(number == want[rows_at, :], 1.0, 0.0).astype(jnp.bfloat16)
        for piece in range(4):
            c = pl.ds(piece * (width // 4), width // 4)
            out[rows_at, c] = jnp.dot(pick, traces[:, c], preferred_element_type=jnp.float32).astype(jnp.bfloat16)

    def drain(k, _):
        @pl.when(j < rows - 1)
        def _():
            upper(k).wait_send()

        @pl.when(i < cols - 1)
        def _():
            right(k).wait_send()

        return 0

    lax.fori_loop(0, chunks, drain, 0)


def body(trace_op, src_blocks, src_dest, src_shot, ret_shot, ret_count):
    cols = lax.axis_size("gx")
    rows = lax.axis_size("gy")
    ndev = cols * rows
    blk, width = src_blocks.shape
    shots = 2048
    scap = max(2, 2 * blk // ndev)
    dest = src_dest[:, 0]
    hits = (dest[:, None] == jnp.arange(ndev, dtype=jnp.int32)[None, :]).astype(jnp.int32)
    ranks = jnp.sum((jnp.cumsum(hits, axis=0) - 1) * hits, axis=1)
    target = dest * scap + ranks
    place = jnp.arange(ndev * scap, dtype=jnp.int32)[:, None] == target[None, :]
    packed = jnp.dot(
        place.astype(jnp.bfloat16), src_blocks, preferred_element_type=jnp.float32
    ).astype(jnp.bfloat16)
    slot_shots = jnp.max(jnp.where(place, src_shot[None, :], -1), axis=1)
    recv_blocks = lax.all_to_all(
        packed.reshape(ndev, scap, width), ("gx", "gy"), split_axis=0, concat_axis=0, tiled=True
    ).reshape(ndev * scap, width)
    recv_shots = lax.all_to_all(
        slot_shots.reshape(ndev, scap), ("gx", "gy"), split_axis=0, concat_axis=0, tiled=True
    ).reshape(1, ndev * scap)
    live = jnp.arange(RCAP, dtype=jnp.int32)[None, :] < ret_count.reshape(ndev, 1)
    want = jnp.where(live, ret_shot.reshape(ndev, RCAP), -1).reshape(ndev * RCAP, 1)
    vmem = pl.BlockSpec(memory_space=pltpu.VMEM)
    chunks = shots // CHUNK
    chosen = pl.pallas_call(
        functools.partial(sweep, cols, rows),
        out_shape=jax.ShapeDtypeStruct((ndev * RCAP, width), jnp.bfloat16),
        in_specs=[pl.BlockSpec(memory_space=pl.ANY), vmem, vmem, vmem],
        out_specs=vmem,
        scratch_shapes=[
            pltpu.VMEM((width + ndev * scap, width), jnp.bfloat16),
            pltpu.VMEM((shots, width), jnp.bfloat16),
            pltpu.VMEM((shots, width), jnp.bfloat16),
            pltpu.SemaphoreType.DMA,
            pltpu.SemaphoreType.DMA((chunks,)),
            pltpu.SemaphoreType.DMA((chunks,)),
            pltpu.SemaphoreType.DMA((chunks,)),
            pltpu.SemaphoreType.DMA((chunks,)),
        ],
        compiler_params=pltpu.CompilerParams(has_side_effects=True, vmem_limit_bytes=60 * 1024 * 1024),
    )(trace_op.reshape(width, width), recv_blocks, recv_shots, want)
    arrived = lax.all_to_all(
        chosen.reshape(ndev, RCAP, width), ("gx", "gy"), split_axis=0, concat_axis=0, tiled=True
    )
    return arrived.reshape(1, ndev, RCAP, width)


def solution(mesh):
    in_specs = (
        P("gx", "gy", None, None),
        P(("gx", "gy"), None),
        P(("gx", "gy"), None),
        P(("gx", "gy")),
        P(("gx", "gy"), None, None),
        P(("gx", "gy"), None),
    )
    out_specs = P(("gx", "gy"), None, None, None)
    return jax.shard_map(body, mesh=mesh, in_specs=in_specs, out_specs=out_specs, check_vma=False)
```

time: 722 us -> 321 us (0.44)
  waiting for transfers between devices: 389 us -> 18.3 us
  Pallas kernels: 0 us -> 197 us
  starting transfers between devices: 179 us -> 17.2 us
  matrix products: 70.5 us -> 0.42 us
  blocking collectives: 36.4 us -> 69.8 us
  local copies, waits for them, and re-layouts: 32.7 us -> 9.14 us
    ppermute x60 -> x0, waiting for transfers between devices: 376 us -> none  [shifted(): return lax.ppermute(array, axis, pairs)]
    pallas_call x0 -> x1, Pallas kernels: none -> 197 us  [body(): pl.pallas_call(functools.partial(sweep, cols, rows), out_shape=jax.ShapeD...]
    ppermute x60 -> x0, starting transfers between devices: 162 us -> none  [shifted(): return lax.ppermute(array, axis, pairs)]
    dot_general x17 -> x0, matrix products: 70.1 us -> none  [the longest x8 32.1 us: compute(): jnp.dot(lower, lower_rows, preferred_element_type=jnp.float32)]
    all_to_all x1, blocking collectives: 36.4 us -> 69.8 us  [body(): lax.all_to_all(chosen.reshape(ndev, RCAP, width), ('gx', 'gy'), split_axi...]
    gather x2 -> x0, local copies, waits for them, and re-layouts: 11.1 us -> none  [body(): chosen = jnp.take(traces, wanted, axis=0)]
    slice x31 -> x0, local copies, waits for them, and re-layouts: 8.3 us -> none  [the longest x1 6.02 us: body(): lower_rows = operator[face:]]
  transfers between devices with their start and end apart: 62 -> 2, of which waited for: 56 -> 2; matrix products, arithmetic and copies ran while one was open for 2% -> 2% of each run, Pallas kernels for 0% -> 0%
where the time goes in v1:
time: 321 us; the launch traced here: 317 us
  Pallas kernels  197 us (61%)
  blocking collectives  69.8 us (22%)
  waiting for transfers between devices  18.3 us (6%)
  starting transfers between devices  17.2 us (5%)
  local copies, waits for them, and re-layouts  9.14 us (3%)
  other arithmetic  4.91 us (2%)
    pallas_call x1, Pallas kernels, body(): pl.pallas_call(functools.partial(sweep, cols, rows), out_shape=jax.ShapeD...  197 us
    all_to_all x1, blocking collectives, body(): lax.all_to_all(chosen.reshape(ndev, RCAP, width), ('gx', 'gy'), split_axi...  69.8 us
    all_to_all x1, waiting for transfers between devices, body(): lax.all_to_all(packed.reshape(ndev, scap, width), ('gx', 'gy'), split_axi...  13.3 us
    all_to_all x1, starting transfers between devices, body(): lax.all_to_all(slot_shots.reshape(ndev, scap), ('gx', 'gy'), split_axis=0...  10.1 us
    all_to_all x1, starting transfers between devices, body(): lax.all_to_all(packed.reshape(ndev, scap, width), ('gx', 'gy'), split_axi...  7.07 us
  transfers between devices with their start and end apart: 2, of which 2 were waited for; matrix products, arithmetic and copies ran while one was open for 2% of the time, Pallas kernels for 0%

profile of v1, /device:TPU:97, one launch (start us, length us, event | category | flops | bytes accessed | tf_op | source)
XLA Modules:
  0.0 316.7 jit_solution(2085571439976889268)
XLA Ops:
  0.0 0.8 fusion.1
  0.8 0.2 reduce_window_sum.11
  1.0 0.8 select_reduce_fusion.1
  1.8 0.7 multiply_add_fusion
  2.5 0.8 select_reduce_fusion
  3.2 0.8 all_to_all.13
  4.0 10.1 %all-to-all-start.1 = ((s32[128,1,2]{2,1,0:T(1,128)}), s32[128,1,2]{2,1,0:T(1,128)S(1)}, u32[]{:S(2)}, u32[]{:S(2)}) async-start(s32[128,1,2]{2,1,0:T(1,128)} %bitcast.2), calls=%async_computation.1 | async-start | bytes 131072 | tf_op jit(solution)/shard_map/all_to_all | solution.py:128
  14.2 0.4 convolution_convert_fusion
  14.6 1.5 reshape.71
  16.1 5.1 %all-to-all-done.1 = s32[128,1,2]{2,1,0:T(1,128)S(1)} async-done(((s32[128,1,2]{2,1,0:T(1,128)}), s32[128,1,2]{2,1,0:T(1,128)S(1)}, u32[]{:S(2)}, u32[]{:S(2)}) %all-to-all-start.1) | async-done | bytes 1056 | tf_op jit(solution)/shard_map/all_to_all | solution.py:128
  21.2 7.1 %all-to-all-start = ((bf16[128,2,2048]{2,1,0:T(2,128)(2,1)}), bf16[128,2,2048]{2,1,0:T(2,128)(2,1)S(1)}, u32[]{:S(2)}, u32[]{:S(2)}) async-start(bf16[128,2,2048]{2,1,0:T(2,128)(2,1)} %reshape.71), calls=%async_computation | async-start | bytes 2097152 | tf_op jit(solution)/shard_map/all_to_all | solution.py:125
  28.4 0.1 lt.30
  28.5 0.1 copy.16
  28.7 0.1 reshape.77
  28.8 0.8 broadcast_select_fusion.want
  29.5 0.6 broadcast.29
  30.1 0.8 reduce.3
  31.0 0.7 reshape.73.shots
  31.6 13.3 %all-to-all-done = bf16[128,2,2048]{2,1,0:T(2,128)(2,1)S(1)} async-done(((bf16[128,2,2048]{2,1,0:T(2,128)(2,1)}), bf16[128,2,2048]{2,1,0:T(2,128)(2,1)S(1)}, u32[]{:S(2)}, u32[]{:S(2)}) %all-to-all-start) | async-done | bytes 1048608 | tf_op jit(solution)/shard_map/all_to_all | solution.py:125
  44.9 1.2 reshape.72.blocks
  46.1 196.7 %shard_map.64 = bf16[512,2048]{1,0:T(8,128)(2,1)} custom-call(bf16[2048,2048]{1,0:T(8,128)(2,1)} %bitcast.7, bf16[256,2048]{1,0:T(8,128)(2,1)} %reshape.72.blocks, s32[1,256]{1,0:T(1,128)} %reshape.73.shots, s32[512,1]{1,0:T(8,128)} %broadcast_select_fusion.want), custom_call_target="tpu_custom_call" | custom-call | tf_op jit(solution)/shard_map/pallas_call | solution.py:135
  242.8 2.7 reshape.75
  245.6 69.8 %all_to_all.19 = bf16[128,4,2048]{2,1,0:T(4,128)(2,1)S(1)} all-to-all(bf16[128,4,2048]{2,1,0:T(4,128)(2,1)S(1)} %reshape.75), channel_id=1, replica_groups=mesh['gx'=8,'gy'=16] {'gx','gy'}, dimensions={0} | all-to-all | bytes 4194304 | tf_op jit(solution)/shard_map/all_to_all | solution.py:152
  315.4 1.3 copy.20
  (7 shorter events, 0.1 us)
Async XLA Ops:
  0.0 14.2 %copy-start = (bf16[128,2048]{1,0:T(8,128)(2,1)S(1)}, bf16[128,2048]{1,0:T(8,128)(2,1)}, u32[]{:S(2)}) copy-start(bf16[128,2048]{1,0:T(8,128)(2,1)} %param.7) | copy-start | bytes 1572868
  4.0 17.2 %all-to-all-start.1 = ((s32[128,1,2]{2,1,0:T(1,128)}), s32[128,1,2]{2,1,0:T(1,128)S(1)}, u32[]{:S(2)}, u32[]{:S(2)}) async-start(s32[128,1,2]{2,1,0:T(1,128)} %bitcast.2), calls=%async_computation.1 | async-start | bytes 131072 | tf_op jit(solution)/shard_map/all_to_all | solution.py:128
  14.6 13.7 %copy-start.2 = (s32[1,128]{1,0:T(1,128)S(1)}, s32[1,128]{1,0:T(1,128)}, u32[]{:S(2)}) copy-start(s32[1,128]{1,0:T(1,128)} %param.11) | copy-start | bytes 1540
  14.6 13.9 %copy-start.1 = (s32[1,128,4]{1,2,0:T(4,128)S(1)}, s32[1,128,4]{1,2,0:T(4,128)}, u32[]{:S(2)}) copy-start(s32[1,128,4]{1,2,0:T(4,128)} %param.10) | copy-start | bytes 6148
  21.2 23.7 %all-to-all-start = ((bf16[128,2,2048]{2,1,0:T(2,128)(2,1)}), bf16[128,2,2048]{2,1,0:T(2,128)(2,1)S(1)}, u32[]{:S(2)}, u32[]{:S(2)}) async-start(bf16[128,2,2048]{2,1,0:T(2,128)(2,1)} %reshape.71), calls=%async_computation | async-start | bytes 2097152 | tf_op jit(solution)/shard_map/all_to_all | solution.py:125

commit v2 on v1

v2 whole, which is shorter than its diff:
```python
import functools

import jax
import jax.numpy as jnp
from jax import lax
from jax.experimental import pallas as pl
from jax.experimental.pallas import tpu as pltpu
from jax.sharding import PartitionSpec as P

MESH = pl.DeviceIdType.MESH
CHUNK = 32
RCAP = 4
LANES = 128


def mega(cols, rows, w_hbm, src, dest_c, dest_r, shot_r, want, out,
         w, xbuf, traces, sbuf, rbuf, gbuf, shots, wsem, ssem, rsem, lsem, gsem, osem, psem,
         send_r, recv_r, send_u, recv_u):
    i = lax.axis_index("gx")
    j = lax.axis_index("gy")
    ndev = cols * rows
    me = i * rows + j
    total, width = traces.shape
    face = width // 2
    scap = sbuf.shape[1]
    slots = ndev * scap
    blk = src.shape[0]
    chunks = total // CHUNK
    load = pltpu.make_async_copy(w_hbm, w.at[pl.ds(0, width)], wsem)
    load.start()

    same = dest_c[...] == dest_r[...]
    earlier = lax.broadcasted_iota(jnp.int32, (blk, blk), 0) < lax.broadcasted_iota(jnp.int32, (blk, blk), 1)
    rank = jnp.sum(jnp.where(same & earlier, 1, 0), axis=0, keepdims=True)
    target = dest_r[...] * scap + rank
    place = lax.broadcasted_iota(jnp.int32, (slots, blk), 0) == target
    tag = jnp.sum(jnp.where(place, shot_r[...] + 1, 0), axis=1, keepdims=True)
    lane = lax.broadcasted_iota(jnp.int32, (slots, LANES), 1)
    extra = jnp.where(lane == 0, lax.shift_right_logical(tag, 6), jnp.where(lane == 1, tag & 63, 0))
    place = jnp.where(place, 1.0, 0.0).astype(jnp.bfloat16)
    for c in range(0, width, 512):
        part = jnp.dot(place, src[:, c:c + 512], preferred_element_type=jnp.float32).astype(jnp.bfloat16)
        sbuf[:, :, c:c + 512] = part.reshape(ndev, scap, 512)
    sbuf[:, :, width:] = extra.astype(jnp.float32).astype(jnp.bfloat16).reshape(ndev, scap, LANES)

    def block(a, b):
        return pltpu.make_async_remote_copy(
            src_ref=sbuf.at[a * rows + b], dst_ref=rbuf.at[me], send_sem=ssem, recv_sem=rsem,
            device_id=(a, b), device_id_type=MESH,
        )

    def post(t, _):
        a = lax.rem(t + i, cols)
        b = t // cols - a

        @pl.when((b >= 0) & (b < rows) & ((a != i) | (b != j)))
        def _():
            block(a, b).start()

        return 0

    lax.fori_loop(0, (cols + rows - 1) * cols, post, 0)
    own = pltpu.make_async_copy(sbuf.at[me], rbuf.at[me], lsem)
    own.start()

    @pl.when(i == 0)
    def _():
        xbuf[:, :face] = jnp.zeros((total, face), jnp.bfloat16)

    @pl.when(j == 0)
    def _():
        xbuf[:, face:] = jnp.zeros((total, face), jnp.bfloat16)

    own.wait()
    pltpu.make_async_copy(rbuf.at[pl.ds(0, ndev - 1)], rbuf.at[pl.ds(0, ndev - 1)], rsem).wait()
    for c in range(0, width, 512):
        w[width:, c:c + 512] = rbuf[:, :, c:c + 512].reshape(slots, 512)
    code = rbuf[:, :, width:].reshape(slots, LANES).astype(jnp.float32)
    code = jnp.transpose(code)
    shots[...] = (code[0:1, :] * 64.0 + code[1:2, :] - 1.0).astype(jnp.int32)
    load.wait()

    def right(k):
        at = pl.ds(pl.multiple_of(k * CHUNK, CHUNK), CHUNK)
        return pltpu.make_async_remote_copy(
            src_ref=traces.at[at, pl.ds(0, face)],
            dst_ref=xbuf.at[at, pl.ds(0, face)],
            send_sem=send_r.at[k],
            recv_sem=recv_r.at[k],
            device_id=(lax.rem(i + 1, cols), j),
            device_id_type=MESH,
        )

    def upper(k):
        at = pl.ds(pl.multiple_of(k * CHUNK, CHUNK), CHUNK)
        return pltpu.make_async_remote_copy(
            src_ref=traces.at[at, pl.ds(face, face)],
            dst_ref=xbuf.at[at, pl.ds(face, face)],
            send_sem=send_u.at[k],
            recv_sem=recv_u.at[k],
            device_id=(i, lax.rem(j + 1, rows)),
            device_id_type=MESH,
        )

    def step(k, _):
        at = pl.ds(pl.multiple_of(k * CHUNK, CHUNK), CHUNK)
        number = lax.broadcasted_iota(jnp.int32, (CHUNK, slots), 0) + k * CHUNK
        pick = jnp.where(number == shots[...], 1.0, 0.0).astype(jnp.bfloat16)

        @pl.when(i > 0)
        def _():
            right(k).wait_recv()

        @pl.when(j > 0)
        def _():
            upper(k).wait_recv()

        x = jnp.concatenate([xbuf[at, :], pick], axis=1)
        traces[at, face:] = jnp.dot(x, w[:, face:], preferred_element_type=jnp.float32).astype(jnp.bfloat16)

        @pl.when(j < rows - 1)
        def _():
            upper(k).start()

        traces[at, :face] = jnp.dot(x, w[:, :face], preferred_element_type=jnp.float32).astype(jnp.bfloat16)

        @pl.when(i < cols - 1)
        def _():
            right(k).start()

        return 0

    lax.fori_loop(0, chunks, step, 0)

    def answer(o):
        return pltpu.make_async_remote_copy(
            src_ref=gbuf.at[o], dst_ref=out.at[me], send_sem=gsem, recv_sem=osem,
            device_id=(o // rows, lax.rem(o, rows)), device_id_type=MESH,
        )

    owners = 32
    parts = ndev // owners
    number = lax.broadcasted_iota(jnp.int32, (owners * RCAP, total), 1)

    def gather(t, _):
        part = lax.rem(t + me // owners, parts)
        rows_at = pl.ds(pl.multiple_of(part * owners * RCAP, owners * RCAP), owners * RCAP)
        base = pl.multiple_of(part * owners, owners)
        pick = jnp.where(number == want[rows_at, :], 1.0, 0.0).astype(jnp.bfloat16)
        for c in range(0, width, 512):
            got = jnp.dot(pick, traces[:, c:c + 512], preferred_element_type=jnp.float32).astype(jnp.bfloat16)
            gbuf[pl.ds(base, owners), :, c:c + 512] = got.reshape(owners, RCAP, 512)

        def reply(q, _):
            o = base + lax.rem(q + me, owners)

            @pl.when(o != me)
            def _():
                answer(o).start()

            return 0

        lax.fori_loop(0, owners, reply, 0)
        return 0

    lax.fori_loop(0, parts, gather, 0)
    mine = pltpu.make_async_copy(gbuf.at[me], out.at[me], psem)
    mine.start()

    def drain(k, _):
        @pl.when(j < rows - 1)
        def _():
            upper(k).wait_send()

        @pl.when(i < cols - 1)
        def _():
            right(k).wait_send()

        return 0

    lax.fori_loop(0, chunks, drain, 0)
    most = pl.ds(0, ndev - 1)
    pltpu.make_async_copy(sbuf.at[most], sbuf.at[most], ssem).wait()
    pltpu.make_async_copy(gbuf.at[most], gbuf.at[most], gsem).wait()
    mine.wait()
    pltpu.make_async_copy(out.at[most], out.at[most], osem).wait()


def body(trace_op, src_blocks, src_dest, src_shot, ret_shot, ret_count):
    cols = lax.axis_size("gx")
    rows = lax.axis_size("gy")
    ndev = cols * rows
    blk, width = src_blocks.shape
    total = 2048
    scap = 2
    live = jnp.arange(RCAP, dtype=jnp.int32)[None, :] < ret_count.reshape(ndev, 1)
    want = jnp.where(live, ret_shot.reshape(ndev, RCAP), -1).reshape(ndev * RCAP, 1)
    vmem = pl.BlockSpec(memory_space=pltpu.VMEM)
    hbm = pl.BlockSpec(memory_space=pl.ANY)
    chunks = total // CHUNK
    dma = pltpu.SemaphoreType.DMA
    arrived = pl.pallas_call(
        functools.partial(mega, cols, rows),
        out_shape=jax.ShapeDtypeStruct((ndev, RCAP, width), jnp.bfloat16),
        in_specs=[hbm, vmem, vmem, vmem, vmem, vmem],
        out_specs=hbm,
        scratch_shapes=[
            pltpu.VMEM((width + ndev * scap, width), jnp.bfloat16),
            pltpu.VMEM((total, width), jnp.bfloat16),
            pltpu.VMEM((total, width), jnp.bfloat16),
            pltpu.VMEM((ndev, scap, width + LANES), jnp.bfloat16),
            pltpu.VMEM((ndev, scap, width + LANES), jnp.bfloat16),
            pltpu.VMEM((ndev, RCAP, width), jnp.bfloat16),
            pltpu.VMEM((1, ndev * scap), jnp.int32),
            dma, dma, dma, dma, dma, dma, dma,
            dma((chunks,)), dma((chunks,)), dma((chunks,)), dma((chunks,)),
        ],
        compiler_params=pltpu.CompilerParams(has_side_effects=True, vmem_limit_bytes=60 * 1024 * 1024),
    )(
        trace_op.reshape(width, width),
        src_blocks,
        src_dest,
        src_dest.reshape(1, blk),
        src_shot.reshape(1, blk),
        want,
    )
    return arrived.reshape(1, ndev, RCAP, width)


def solution(mesh):
    in_specs = (
        P("gx", "gy", None, None),
        P(("gx", "gy"), None),
        P(("gx", "gy"), None),
        P(("gx", "gy")),
        P(("gx", "gy"), None, None),
        P(("gx", "gy"), None),
    )
    out_specs = P(("gx", "gy"), None, None, None)
    return jax.shard_map(body, mesh=mesh, in_specs=in_specs, out_specs=out_specs, check_vma=False)
```

time: 321 us -> 308 us (0.960)
  the two profiles are of different devices: /device:TPU:97 before, /device:TPU:19 now
where the time goes in v2:
time: 308 us
  Pallas kernels  300 us (97%)
  local copies, waits for them, and re-layouts  6.34 us (2%)
    pallas_call x1, Pallas kernels, body(): pl.pallas_call(functools.partial(mega, cols, rows), out_shape=jax.ShapeDt...  300 us

profile of v2, /device:TPU:19, one launch (start us, length us, event | category | flops | bytes accessed | tf_op | source)
XLA Modules:
  0.0 308.3 jit_solution(10112563428298843750)
XLA Ops:
  0.0 0.7 iota_compare_fusion
  0.7 0.1 lt.30
  0.9 0.8 copy.9
  1.7 1.4 copy.12.dest_c
  3.1 0.1 reshape.55
  3.2 0.7 broadcast_select_fusion.want
  3.9 300.4 %shard_map.64 = bf16[128,4,2048]{2,1,0:T(4,128)(2,1)} custom-call(bf16[2048,2048]{1,0:T(8,128)(2,1)} %bitcast.5, bf16[128,2048]{1,0:T(8,128)(2,1)} %src.1, s32[128,1]{1,0:T(8,128)} %copy.12.dest_c, s32[1,128]{1,0:T(1,128)} %bitcast.7, s32[1,128]{1,0:T(1,128)} %bitcast.8, s32[512,1]{1,0:T(8,128)} %broadcast_select_fusion.want), custom_call_target="tpu_custom_call" | custom-call | tf_op jit(solution)/shard_map/pallas_call | solution.py:202
  304.3 3.9 %copy.14 = bf16[1,128,4,2048]{3,2,1,0:T(4,128)(2,1)} copy(bf16[1,128,4,2048]{3,2,1,0:T(4,128)(2,1)} %bitcast.6) | data formatting | bytes 4194304

commit v3 on v2

--- a/solution.py
+++ b/solution.py
@@ -8,28 +8,32 @@
 from jax.sharding import PartitionSpec as P
 
 MESH = pl.DeviceIdType.MESH
-CHUNK = 32
+CHUNK = 48
+SPAN = 384
+MARK = 3
+BAND = 4
 RCAP = 4
 LANES = 128
 
 
-def mega(cols, rows, w_hbm, src, dest_c, dest_r, shot_r, want, out,
-         w, xbuf, traces, sbuf, rbuf, gbuf, shots, wsem, ssem, rsem, lsem, gsem, osem, psem,
+def mega(cols, rows, total, w_hbm, src, dest_r, shot_r, ret, count, out,
+         w, xbuf, traces, sbuf, rbuf, gbuf, acc, want, shots, gate, wsem, ssem, rsem, lsem, gsem, osem, psem,
          send_r, recv_r, send_u, recv_u):
     i = lax.axis_index("gx")
     j = lax.axis_index("gy")
     ndev = cols * rows
     me = i * rows + j
-    total, width = traces.shape
+    padded, width = traces.shape
     face = width // 2
     scap = sbuf.shape[1]
     slots = ndev * scap
     blk = src.shape[0]
-    chunks = total // CHUNK
+    chunks = padded // CHUNK
     load = pltpu.make_async_copy(w_hbm, w.at[pl.ds(0, width)], wsem)
     load.start()
 
-    same = dest_c[...] == dest_r[...]
+    dest_c = jnp.transpose(jnp.broadcast_to(dest_r[...].astype(jnp.float32), (blk, blk)))
+    same = dest_c == dest_r[...].astype(jnp.float32)
     earlier = lax.broadcasted_iota(jnp.int32, (blk, blk), 0) < lax.broadcasted_iota(jnp.int32, (blk, blk), 1)
     rank = jnp.sum(jnp.where(same & earlier, 1, 0), axis=0, keepdims=True)
     target = dest_r[...] * scap + rank
@@ -63,13 +67,30 @@
     own = pltpu.make_async_copy(sbuf.at[me], rbuf.at[me], lsem)
     own.start()
 
+    slot = lax.broadcasted_iota(jnp.int32, (RCAP, ndev), 0)
+    asked = jnp.where(slot < count[...], ret[...] + 1, 0)
+    split = jnp.concatenate(
+        [lax.shift_right_logical(asked, 6), asked & 63, jnp.zeros((ndev - 2 * RCAP, ndev), jnp.int32)], axis=0
+    ).astype(jnp.float32)
+    split = jnp.transpose(split).astype(jnp.bfloat16)
+    asks = ndev * RCAP
+    row = lax.broadcasted_iota(jnp.int32, (asks, ndev), 0)
+    lane = lax.broadcasted_iota(jnp.int32, (asks, ndev), 1)
+    place = row // RCAP
+    owner = (place // BAND % cols) * rows + place // (BAND * cols) * BAND + place % BAND
+    spread = jnp.where(lane == owner, 1.0, 0.0).astype(jnp.bfloat16)
+    spread = jnp.dot(spread, split, preferred_element_type=jnp.float32)
+    spread = jnp.where(lane == row % RCAP, spread * 64.0, jnp.where(lane == row % RCAP + RCAP, spread, 0.0))
+    want[...] = jnp.sum(spread, axis=1, keepdims=True).astype(jnp.int32) - 1
+    acc[...] = jnp.zeros_like(acc)
+
     @pl.when(i == 0)
     def _():
-        xbuf[:, :face] = jnp.zeros((total, face), jnp.bfloat16)
+        xbuf[:, :face] = jnp.zeros((padded, face), jnp.bfloat16)
 
     @pl.when(j == 0)
     def _():
-        xbuf[:, face:] = jnp.zeros((total, face), jnp.bfloat16)
+        xbuf[:, face:] = jnp.zeros((padded, face), jnp.bfloat16)
 
     own.wait()
     pltpu.make_async_copy(rbuf.at[pl.ds(0, ndev - 1)], rbuf.at[pl.ds(0, ndev - 1)], rsem).wait()
@@ -128,43 +149,69 @@
         def _():
             right(k).start()
 
+        @pl.when(lax.rem(k, SPAN // CHUNK) == SPAN // CHUNK - 1)
+        def _():
+            first = pl.multiple_of((k // (SPAN // CHUNK)) * SPAN, SPAN)
+            number = lax.broadcasted_iota(jnp.int32, (asks, SPAN), 1) + first
+            pick = jnp.where(number == want[...], 1.0, 0.0).astype(jnp.bfloat16)
+            for c in range(0, width, 256):
+                got = jnp.dot(pick, traces[pl.ds(first, SPAN), c:c + 256], preferred_element_type=jnp.float32)
+                acc[:, c:c + 256] += got.astype(jnp.bfloat16)
+
         return 0
 
     lax.fori_loop(0, chunks, step, 0)
 
-    def answer(o):
-        return pltpu.make_async_remote_copy(
-            src_ref=gbuf.at[o], dst_ref=out.at[me], send_sem=gsem, recv_sem=osem,
-            device_id=(o // rows, lax.rem(o, rows)), device_id_type=MESH,
-        )
-
-    owners = 32
-    parts = ndev // owners
-    number = lax.broadcasted_iota(jnp.int32, (owners * RCAP, total), 1)
-
-    def gather(t, _):
-        part = lax.rem(t + me // owners, parts)
-        rows_at = pl.ds(pl.multiple_of(part * owners * RCAP, owners * RCAP), owners * RCAP)
-        base = pl.multiple_of(part * owners, owners)
+    def answer(q, a, b):
+        return pltpu.make_async_remote_copy(
+            src_ref=gbuf.at[q], dst_ref=out.at[me], send_sem=gsem, recv_sem=osem,
+            device_id=(a, b), device_id_type=MESH,
+        )
+
+    @pl.when((i == MARK) & (lax.rem(j, BAND) == BAND - 1))
+    def _():
+        def tell(p, _):
+            @pl.when(p != me)
+            def _():
+                pl.semaphore_signal(
+                    gate.at[j // BAND], inc=1, device_id=(p // rows, lax.rem(p, rows)), device_id_type=MESH
+                )
+
+            return 0
+
+        lax.fori_loop(0, ndev, tell, 0)
+        pl.semaphore_signal(gate.at[j // BAND], inc=1)
+
+    last = total // SPAN * SPAN
+    owners = BAND * cols
+    number = lax.broadcasted_iota(jnp.int32, (owners * RCAP, total - last), 1) + last
+
+    def finish(g, _):
+        rows_at = pl.ds(pl.multiple_of(g * owners * RCAP, owners * RCAP), owners * RCAP)
         pick = jnp.where(number == want[rows_at, :], 1.0, 0.0).astype(jnp.bfloat16)
         for c in range(0, width, 512):
-            got = jnp.dot(pick, traces[:, c:c + 512], preferred_element_type=jnp.float32).astype(jnp.bfloat16)
-            gbuf[pl.ds(base, owners), :, c:c + 512] = got.reshape(owners, RCAP, 512)
+            got = jnp.dot(pick, traces[last:total, c:c + 512], preferred_element_type=jnp.float32).astype(jnp.bfloat16)
+            got = got + acc[rows_at, c:c + 512]
+            gbuf[pl.ds(pl.multiple_of(g * owners, owners), owners), :, c:c + 512] = got.reshape(owners, RCAP, 512)
+        pl.semaphore_wait(gate.at[g], 1)
 
         def reply(q, _):
-            o = base + lax.rem(q + me, owners)
-
-            @pl.when(o != me)
+            t = lax.rem(q + me, owners)
+            a = t // BAND
+            b = g * BAND + lax.rem(t, BAND)
+
+            @pl.when((a != i) | (b != j))
             def _():
-                answer(o).start()
+                answer(g * owners + t, a, b).start()
 
             return 0
 
         lax.fori_loop(0, owners, reply, 0)
         return 0
 
-    lax.fori_loop(0, parts, gather, 0)
-    mine = pltpu.make_async_copy(gbuf.at[me], out.at[me], psem)
+    lax.fori_loop(0, rows // BAND, finish, 0)
+    home = (j // BAND) * owners + i * BAND + lax.rem(j, BAND)
+    mine = pltpu.make_async_copy(gbuf.at[home], out.at[me], psem)
     mine.start()
 
     def drain(k, _):
@@ -193,25 +240,27 @@
     blk, width = src_blocks.shape
     total = 2048
     scap = 2
-    live = jnp.arange(RCAP, dtype=jnp.int32)[None, :] < ret_count.reshape(ndev, 1)
-    want = jnp.where(live, ret_shot.reshape(ndev, RCAP), -1).reshape(ndev * RCAP, 1)
     vmem = pl.BlockSpec(memory_space=pltpu.VMEM)
     hbm = pl.BlockSpec(memory_space=pl.ANY)
-    chunks = total // CHUNK
+    chunks = pl.cdiv(total, CHUNK)
+    padded = chunks * CHUNK
     dma = pltpu.SemaphoreType.DMA
     arrived = pl.pallas_call(
-        functools.partial(mega, cols, rows),
+        functools.partial(mega, cols, rows, total),
         out_shape=jax.ShapeDtypeStruct((ndev, RCAP, width), jnp.bfloat16),
         in_specs=[hbm, vmem, vmem, vmem, vmem, vmem],
         out_specs=hbm,
         scratch_shapes=[
             pltpu.VMEM((width + ndev * scap, width), jnp.bfloat16),
-            pltpu.VMEM((total, width), jnp.bfloat16),
-            pltpu.VMEM((total, width), jnp.bfloat16),
+            pltpu.VMEM((padded, width), jnp.bfloat16),
+            pltpu.VMEM((padded, width), jnp.bfloat16),
             pltpu.VMEM((ndev, scap, width + LANES), jnp.bfloat16),
             pltpu.VMEM((ndev, scap, width + LANES), jnp.bfloat16),
             pltpu.VMEM((ndev, RCAP, width), jnp.bfloat16),
+            pltpu.VMEM((ndev * RCAP, width), jnp.bfloat16),
+            pltpu.VMEM((ndev * RCAP, 1), jnp.int32),
             pltpu.VMEM((1, ndev * scap), jnp.int32),
+            pltpu.SemaphoreType.REGULAR((rows // BAND,)),
             dma, dma, dma, dma, dma, dma, dma,
             dma((chunks,)), dma((chunks,)), dma((chunks,)), dma((chunks,)),
         ],
@@ -219,10 +268,10 @@
     )(
         trace_op.reshape(width, width),
         src_blocks,
-        src_dest,
         src_dest.reshape(1, blk),
         src_shot.reshape(1, blk),
-        want,
+        ret_shot.reshape(ndev, RCAP).T,
+        ret_count.reshape(1, ndev),
     )
     return arrived.reshape(1, ndev, RCAP, width)
 

time: 308 us -> 271 us (0.88)
  the two profiles are of different devices: /device:TPU:19 before, /device:TPU:97 now
where the time goes in v3:
time: 271 us
  Pallas kernels  267 us (99%)
  local copies, waits for them, and re-layouts  3.92 us (1%)
    pallas_call x1, Pallas kernels, body(): pl.pallas_call(functools.partial(mega, cols, rows, total), out_shape=jax....  267 us

profile of v3, /device:TPU:97, one launch (start us, length us, event | category | flops | bytes accessed | tf_op | source)
XLA Modules:
  0.0 271.2 jit_solution(17390724823423230566)
XLA Ops:
  0.0 267.3 %shard_map.64 = bf16[128,4,2048]{2,1,0:T(4,128)(2,1)} custom-call(bf16[2048,2048]{1,0:T(8,128)(2,1)} %bitcast.8, bf16[128,2048]{1,0:T(8,128)(2,1)} %src.1, s32[1,128]{1,0:T(1,128)} %bitcast.10, s32[1,128]{1,0:T(1,128)} %bitcast.11, s32[4,128]{1,0:T(4,128)} %bitcast.9, s32[1,128]{1,0:T(1,128)} %count.1), custom_call_target="tpu_custom_call" | custom-call | tf_op jit(solution)/shard_map/pallas_call | solution.py:248
  267.3 3.9 %copy.8 = bf16[1,128,4,2048]{3,2,1,0:T(4,128)(2,1)} copy(bf16[1,128,4,2048]{3,2,1,0:T(4,128)(2,1)} %bitcast.7) | data formatting | bytes 4194304

commit v4 on v3

--- a/solution.py
+++ b/solution.py
@@ -10,14 +10,14 @@
 MESH = pl.DeviceIdType.MESH
 CHUNK = 48
 SPAN = 384
-MARK = 3
+MARK = 5
 BAND = 4
 RCAP = 4
 LANES = 128
 
 
 def mega(cols, rows, total, w_hbm, src, dest_r, shot_r, ret, count, out,
-         w, xbuf, traces, sbuf, rbuf, gbuf, acc, want, shots, gate, wsem, ssem, rsem, lsem, gsem, osem, psem,
+         w, xbuf, traces, sbuf, rbuf, gbuf, acc, want, shots, held, gate, wsem, ssem, rsem, lsem, gsem, osem, psem,
          send_r, recv_r, send_u, recv_u):
     i = lax.axis_index("gx")
     j = lax.axis_index("gy")
@@ -31,6 +31,16 @@
     chunks = padded // CHUNK
     load = pltpu.make_async_copy(w_hbm, w.at[pl.ds(0, width)], wsem)
     load.start()
+    barrier = pltpu.get_barrier_semaphore()
+
+    def greet(p, _):
+        @pl.when(p != me)
+        def _():
+            pl.semaphore_signal(barrier, inc=1, device_id=(p // rows, lax.rem(p, rows)), device_id_type=MESH)
+
+        return 0
+
+    lax.fori_loop(0, ndev, greet, 0)
 
     dest_c = jnp.transpose(jnp.broadcast_to(dest_r[...].astype(jnp.float32), (blk, blk)))
     same = dest_c == dest_r[...].astype(jnp.float32)
@@ -46,6 +56,8 @@
         part = jnp.dot(place, src[:, c:c + 512], preferred_element_type=jnp.float32).astype(jnp.bfloat16)
         sbuf[:, :, c:c + 512] = part.reshape(ndev, scap, 512)
     sbuf[:, :, width:] = extra.astype(jnp.float32).astype(jnp.bfloat16).reshape(ndev, scap, LANES)
+
+    pl.semaphore_wait(barrier, ndev - 1)
 
     def block(a, b):
         return pltpu.make_async_remote_copy(
@@ -128,6 +140,9 @@
         number = lax.broadcasted_iota(jnp.int32, (CHUNK, slots), 0) + k * CHUNK
         pick = jnp.where(number == shots[...], 1.0, 0.0).astype(jnp.bfloat16)
 
+        extra = jnp.dot(pick, w[width:, :], preferred_element_type=jnp.float32)
+        held[...] = extra
+
         @pl.when(i > 0)
         def _():
             right(k).wait_recv()
@@ -136,14 +151,16 @@
         def _():
             upper(k).wait_recv()
 
-        x = jnp.concatenate([xbuf[at, :], pick], axis=1)
-        traces[at, face:] = jnp.dot(x, w[:, face:], preferred_element_type=jnp.float32).astype(jnp.bfloat16)
+        x = xbuf[at, :]
+        term = jnp.dot(x, w[:width, face:], preferred_element_type=jnp.float32) + held[:, face:]
+        traces[at, face:] = term.astype(jnp.bfloat16)
 
         @pl.when(j < rows - 1)
         def _():
             upper(k).start()
 
-        traces[at, :face] = jnp.dot(x, w[:, :face], preferred_element_type=jnp.float32).astype(jnp.bfloat16)
+        term = jnp.dot(x, w[:width, :face], preferred_element_type=jnp.float32) + held[:, :face]
+        traces[at, :face] = term.astype(jnp.bfloat16)
 
         @pl.when(i < cols - 1)
         def _():
@@ -186,6 +203,8 @@
     owners = BAND * cols
     number = lax.broadcasted_iota(jnp.int32, (owners * RCAP, total - last), 1) + last
 
+    pl.semaphore_wait(gate.at[j // BAND], 1)
+
     def finish(g, _):
         rows_at = pl.ds(pl.multiple_of(g * owners * RCAP, owners * RCAP), owners * RCAP)
         pick = jnp.where(number == want[rows_at, :], 1.0, 0.0).astype(jnp.bfloat16)
@@ -193,7 +212,10 @@
             got = jnp.dot(pick, traces[last:total, c:c + 512], preferred_element_type=jnp.float32).astype(jnp.bfloat16)
             got = got + acc[rows_at, c:c + 512]
             gbuf[pl.ds(pl.multiple_of(g * owners, owners), owners), :, c:c + 512] = got.reshape(owners, RCAP, 512)
-        pl.semaphore_wait(gate.at[g], 1)
+        @pl.when(g != j // BAND)
+        def _():
+            pl.semaphore_wait(gate.at[g], 1)
+
 
         def reply(q, _):
             t = lax.rem(q + me, owners)
@@ -248,7 +270,7 @@
     arrived = pl.pallas_call(
         functools.partial(mega, cols, rows, total),
         out_shape=jax.ShapeDtypeStruct((ndev, RCAP, width), jnp.bfloat16),
-        in_specs=[hbm, vmem, vmem, vmem, vmem, vmem],
+        in_specs=[pl.BlockSpec(memory_space=pltpu.HBM), vmem, vmem, vmem, vmem, vmem],
         out_specs=hbm,
         scratch_shapes=[
             pltpu.VMEM((width + ndev * scap, width), jnp.bfloat16),
@@ -260,11 +282,12 @@
             pltpu.VMEM((ndev * RCAP, width), jnp.bfloat16),
             pltpu.VMEM((ndev * RCAP, 1), jnp.int32),
             pltpu.VMEM((1, ndev * scap), jnp.int32),
+            pltpu.VMEM((CHUNK, width), jnp.float32),
             pltpu.SemaphoreType.REGULAR((rows // BAND,)),
             dma, dma, dma, dma, dma, dma, dma,
             dma((chunks,)), dma((chunks,)), dma((chunks,)), dma((chunks,)),
         ],
-        compiler_params=pltpu.CompilerParams(has_side_effects=True, vmem_limit_bytes=60 * 1024 * 1024),
+        compiler_params=pltpu.CompilerParams(has_side_effects=True, collective_id=0, vmem_limit_bytes=50 * 1024 * 1024),
     )(
         trace_op.reshape(width, width),
         src_blocks,

time: 271 us -> 264 us (0.974)
  Pallas kernels: 267 us -> 258 us
    pallas_call x1, Pallas kernels: 267 us -> 258 us  [body(): pl.pallas_call(functools.partial(mega, cols, rows, total), out_shape=jax....]
where the time goes in v4:
time: 264 us; the launch traced here: 263 us
  Pallas kernels  258 us (98%)
  local copies, waits for them, and re-layouts  5.01 us (2%)
    pallas_call x1, Pallas kernels, body(): pl.pallas_call(functools.partial(mega, cols, rows, total), out_shape=jax....  258 us

profile of v4, /device:TPU:97, one launch (start us, length us, event | category | flops | bytes accessed | tf_op | source)
XLA Modules:
  0.0 263.2 jit_solution(386751984967599224)
XLA Ops:
  0.0 0.0 copy-start
  0.0 1.0 copy-done
  1.0 0.0 copy-start.1
  1.0 0.7 copy-done.1
  1.7 0.0 copy-start.2
  1.7 0.7 copy-done.2
  2.4 0.0 copy-start.3
  2.4 0.7 copy-done.3
  3.0 0.0 copy-start.4
  3.0 0.7 copy-done.4
  3.7 258.2 %shard_map.64 = bf16[128,4,2048]{2,1,0:T(4,128)(2,1)S(1)} custom-call(bf16[2048,2048]{1,0:T(8,128)(2,1)} %bitcast.11, bf16[128,2048]{1,0:T(8,128)(2,1)S(1)} %copy-done, s32[1,128]{1,0:T(1,128)S(1)} %bitcast.9, s32[1,128]{1,0:T(1,128)S(1)} %bitcast.10, s32[4,128]{1,0:T(4,128)S(1)} %bitcast.8, s32[1,128]{1,0:T(1,128)S(1)} %copy-done.4), custom_call_target="tpu_custom_call" | custom-call | tf_op jit(solution)/shard_map/pallas_call | solution.py:270
  261.9 1.3 copy.8
Async XLA Ops:
  0.0 1.0 copy-start
  1.0 0.7 copy-start.1
  1.7 0.7 copy-start.2
  2.4 0.7 copy-start.3
  3.0 0.7 copy-start.4
